TPU v7x, 32 devices: a whole 2x2x4 slice. The times are simulated.
32 devices in a mesh: chan: 4 (over y, x), strip: 8 (over z, core).
Axes of the slice: x: 2, y: 2, z: 4, core: 2. Of those that a mesh axis runs over, the one named last changes fastest.
Arguments:
- wave_field: float32 [2, 16, 1536, 1536], P(None, 'chan', 'strip'), may hold values from -6 to 6
- radial_op: float32 [1536, 1536], replicated, may hold values from -1 to 1, as said below
- coupling: float32 [2, 16, 8], replicated, may hold values from -4 to 4
- couple: int32 [16, 8], replicated, may hold values from 0 to 15
- partner: int32 [16], replicated, may hold values from 0 to 15, as said below
- extent: int32 [16], replicated, may hold values from 384 to 1536, as said below
Outputs:
- first_step: float32 [2, 16, 1536, 1536], P(None, None, 'strip', 'chan')
- second_step: float32 [2, 16, 1536, 1536], P(None, None, 'strip', 'chan')
Inputs may be any that keep to these rules, and one draw needn't show every extreme that they name: radial_op is symmetric. partner pairs the channels: partner(partner(c)) == c and partner(c) != c. Each extent is a multiple of 96; some channel has extent 1536 and some 1536 // 4.
All inputs are finite; a program needn't handle non-finite values.
Results may differ from a plain program's by a relative error of at most 0.0003.
Values sent between devices are 32-bit elements; how exact they have to be, the bound alone decides.
A program may use at most 256 MiB of HBM per device.

v0:
```python
import functools

import jax
import jax.numpy as jnp
from jax import lax
from jax.experimental import pallas as pl
from jax.experimental.pallas import tpu as pltpu
from jax.sharding import PartitionSpec as P


def potentials(row_pos, col_pos, count, orders):
    spacing = 8.0 / count
    first = row_pos.astype(jnp.float32) * spacing
    second = col_pos.astype(jnp.float32) * spacing
    lesser = jnp.minimum(first[:, None], second[None, :])
    greater = jnp.maximum(first[:, None], second[None, :])
    root = jnp.sqrt(greater * greater + 1.0)
    result = []
    for order in range(orders):
        result.append(lesser**order / root ** (order + 1))
    return result


def couple_terms(field, image_rows, mirrored, coupling, couple, partner, pots, live):
    total = image_rows + jnp.take(mirrored, partner, axis=1)
    real_part = total[0]
    imag_part = total[1]
    for order in range(len(pots)):
        source = jnp.take(field, couple[:, order], axis=1)
        c_real = coupling[0, :, order][:, None, None]
        c_imag = coupling[1, :, order][:, None, None]
        real_part = real_part + pots[order] * (c_real * source[0] - c_imag * source[1])
        imag_part = imag_part + pots[order] * (c_real * source[1] + c_imag * source[0])
    return jnp.where(live[None], jnp.stack([real_part, imag_part]), 0.0)


def radial_product(radial_op, block):
    return jnp.einsum("ak,pckb->pcab", radial_op, block, precision=lax.Precision.HIGHEST)


def spread_columns(field):
    strips = lax.axis_size("strip")
    local_chans = field.shape[1]
    local_rows = field.shape[2]
    grid = field.shape[3]
    piece = grid // (strips * strips)
    shaped = field.reshape(2, local_chans, local_rows, strips, strips, piece)
    return jnp.transpose(shaped, (0, 1, 2, 4, 3, 5)).reshape(2, local_chans, local_rows, grid)


def spread_tiles(image):
    chans = lax.axis_size("chan")
    strips = lax.axis_size("strip")
    local_chans = image.shape[1]
    grid = image.shape[2]
    width = image.shape[3]
    piece = grid // (strips * strips)
    ratio = strips // chans
    block = grid // chans
    direct_send = image.reshape(2, local_chans, strips, width, chans, ratio * piece)
    direct_send = jnp.transpose(direct_send, (0, 1, 4, 2, 3, 5)).reshape(
        2, local_chans, chans * strips, width, ratio * piece
    )
    mirror_send = image.reshape(2, local_chans, chans, block, strips, piece)
    mirror_send = jnp.transpose(mirror_send, (0, 1, 2, 4, 3, 5)).reshape(
        2, local_chans, chans * strips, block, piece
    )
    direct_got, mirror_got = (
        lax.all_to_all(direct_send, ("chan", "strip"), split_axis=2, concat_axis=2, tiled=True),
        lax.all_to_all(mirror_send, ("chan", "strip"), split_axis=2, concat_axis=2, tiled=True),
    )
    direct_got = direct_got.reshape(2, local_chans, chans, strips, width, ratio, piece)
    direct_tiles = jnp.transpose(direct_got, (0, 2, 1, 4, 5, 3, 6)).reshape(
        2, chans * local_chans, width, block
    )
    mirror_got = mirror_got.reshape(2, local_chans, chans, strips, block, piece)
    mirror_tiles = jnp.transpose(mirror_got, (0, 2, 1, 3, 5, 4)).reshape(
        2, chans * local_chans, width, block
    )
    return (direct_tiles, mirror_tiles)


def general(wave_field, radial_op, coupling, couple, partner, extent):
    chans = lax.axis_size("chan")
    grid = wave_field.shape[3]
    strip_rows = wave_field.shape[2]
    chan_cols = grid // chans
    row_pos = lax.axis_index("strip") * strip_rows + jnp.arange(strip_rows)
    col_pos = lax.axis_index("chan") * chan_cols + jnp.arange(chan_cols)
    pots = potentials(row_pos, col_pos, grid, coupling.shape[2])
    live = (row_pos[None, :, None] < extent[:, None, None]) & (
        col_pos[None, None, :] < extent[:, None, None]
    )

    def radial(block):
        return radial_product(radial_op, block)

    def product_columns(field_rows):
        return radial(lax.all_to_all(field_rows, "strip", split_axis=3, concat_axis=2, tiled=True))

    field_tiles = lax.all_to_all(wave_field, "chan", split_axis=3, concat_axis=1, tiled=True)
    rows_tiles, mirror_tiles = spread_tiles(product_columns(spread_columns(wave_field)))
    first_step = couple_terms(
        field_tiles, rows_tiles, mirror_tiles, coupling, couple, partner, pots, live
    )
    image = product_columns(
        spread_columns(lax.all_to_all(first_step, "chan", split_axis=1, concat_axis=3, tiled=True))
    )
    rows_tiles, mirror_tiles = spread_tiles(image)
    applied = couple_terms(
        first_step, rows_tiles, mirror_tiles, coupling, couple, partner, pots, live
    )
    second_step = 2.0 * applied - field_tiles
    return (first_step, second_step)


MESH = pl.DeviceIdType.MESH
ANY = pl.BlockSpec(memory_space=pl.ANY)


def rem(value, count):
    return lax.rem(value, count)


def greet(others):
    barrier = pltpu.get_barrier_semaphore()
    for other in others:
        pl.semaphore_signal(barrier, inc=1, device_id=other, device_id_type=MESH)
    pl.semaphore_wait(barrier, len(others))


def remote(source, target, send, recv, device):
    return pltpu.make_async_remote_copy(
        src_ref=source,
        dst_ref=target,
        send_sem=send,
        recv_sem=recv,
        device_id=device,
        device_id_type=MESH,
    )


def columns(block, width):
    return pl.ds(pl.multiple_of(block * width, 128), width)


def lines(block, height):
    return pl.ds(pl.multiple_of(block * height, 8), height)


def gather_kernel(chans, strips, x, y, f, zs, zr, cs, cr, ls):
    c = lax.axis_index("chan")
    s = lax.axis_index("strip")
    per = y.shape[0]
    width = y.shape[2]
    rows = x.shape[1]
    ring = [(c, rem(s + d, strips)) for d in range(1, strips)]
    plane = [(rem(c + r, chans), s) for r in range(1, chans)]
    greet(ring + plane)
    copies = []
    for d in range(1, strips):
        t = ring[d - 1][1]
        copies.append(
            remote(
                x.at[pl.ds(rem(t, 2) * per, per), :, columns(t // 2, width)],
                y.at[:, lines(s, rows), :],
                zs.at[d],
                zr.at[d],
                ring[d - 1],
            )
        )
    for r in range(1, chans):
        j = plane[r - 1][0]
        for p in range(2):
            copies.append(
                remote(
                    x.at[pl.ds(p * per, per), :, columns(j, width)],
                    f.at[p * chans + c],
                    cs.at[r * 2 + p],
                    cr.at[r * 2 + p],
                    plane[r - 1],
                )
            )
    copies.append(
        pltpu.make_async_copy(
            x.at[pl.ds(rem(s, 2) * per, per), :, columns(s // 2, width)],
            y.at[:, lines(s, rows), :],
            ls.at[0],
        )
    )
    for p in range(2):
        copies.append(
            pltpu.make_async_copy(
                x.at[pl.ds(p * per, per), :, columns(c, width)], f.at[p * chans + c], ls.at[1 + p]
            )
        )
    for copy in copies:
        copy.start()
    for copy in copies:
        copy.wait()


def image_kernel(chans, strips, i, it, w, mt, dd, zs, zr, ms, mr, fs, fr, ls):
    c = lax.axis_index("chan")
    s = lax.axis_index("strip")
    rows = w.shape[2]
    width = w.shape[3]
    group = s // 2
    member = rem(s, 2)
    ring = [(c, rem(s + d, strips)) for d in range(1, strips)]
    plane = [
        (rem(c + r, chans), group * 2 + rem(member + e, 2))
        for r in range(chans)
        for e in range(2)
    ]
    greet(ring + plane[2:])
    slot = member * chans + c
    hops = []
    for d in range(1, strips):
        t = ring[d - 1][1]
        hops.append(
            remote(i.at[:, lines(t, rows), :], w.at[s], zs.at[d], zr.at[d], ring[d - 1])
        )

    def mirror(k):
        j = plane[k][0]
        m = rem(member + k % 2, 2)
        part = it.at[:, lines(m, rows), columns(j, width)]
        if k == 0:
            return pltpu.make_async_copy(part, mt.at[slot], ls.at[2])
        return remote(part, mt.at[slot], ms.at[k], mr.at[k], plane[k])

    mirrors = [mirror(k) for k in range(2 * chans)]
    for hop in hops:
        hop.start()

    def forward(source, u):
        j = u // 2
        p = rem(u, 2)
        away = rem(j - c + chans, chans)

        @pl.when(away == 0)
        def _():
            pltpu.make_async_copy(source, dd.at[p * chans + c], ls.at[p]).start()

        @pl.when(away != 0)
        def _():
            k = away * 2 + p
            remote(source, dd.at[p * chans + c], fs.at[k], fr.at[k], (j, s)).start()

    forward(i.at[:, lines(s, rows), :], s)
    for copy in mirrors:
        copy.start()
    for d in range(1, strips):
        hops[d - 1].wait_recv()
        u = rem(s - d + strips, strips)
        forward(w.at[u], u)
    for hop in hops:
        hop.wait_send()
    for copy in mirrors:
        copy.wait()
    for p in range(2):
        pltpu.make_async_copy(w.at[0], dd.at[p * chans + c], ls.at[p]).wait()
        for r in range(1, chans):
            k = r * 2 + p
            from_chan = rem(c - r + chans, chans)
            remote(
                w.at[0], dd.at[p * chans + from_chan], fs.at[k], fr.at[k], (rem(c + r, chans), s)
            ).wait()


def back_kernel(chans, strips, v, w, y, cs, cr, zs, zr, ls):
    c = lax.axis_index("chan")
    s = lax.axis_index("strip")
    rows = v.shape[2]
    ring = [(c, rem(s + d, strips)) for d in range(1, strips)]
    plane = [(rem(c + r, chans), s) for r in range(1, chans)]
    greet(ring + plane)
    hops = {}
    for r in range(1, chans):
        j = plane[r - 1][0]
        for p in range(2):
            k = r * 2 + p
            hops[k] = remote(
                v.at[p * chans + j], w.at[p * chans + c], cs.at[k], cr.at[k], plane[r - 1]
            )
            hops[k].start()

    def forward(source, j, p):
        t = j * 2 + p
        away = rem(t - s + strips, strips)

        @pl.when(away == 0)
        def _():
            pltpu.make_async_copy(source, y.at[:, lines(s, rows), :], ls).start()

        @pl.when(away != 0)
        def _():
            remote(
                source, y.at[:, lines(s, rows), :], zs.at[away], zr.at[away], (c, t)
            ).start()

    for p in range(2):
        forward(v.at[p * chans + c], c, p)
    for r in range(1, chans):
        j = rem(c - r + chans, chans)
        for p in range(2):
            hops[r * 2 + p].wait_recv()
            forward(w.at[p * chans + j], j, p)
    for k in hops:
        hops[k].wait_send()
    pltpu.make_async_copy(v.at[0], y.at[:, lines(s, rows), :], ls).wait()
    for d in range(1, strips):
        u = rem(s - d + strips, strips)
        remote(
            v.at[0], y.at[:, lines(u, rows), :], zs.at[d], zr.at[d], (c, rem(s + d, strips))
        ).wait()


def exchange(kernel, ident, outs, sems, *operands):
    chans = lax.axis_size("chan")
    strips = lax.axis_size("strip")
    return pl.pallas_call(
        functools.partial(kernel, chans, strips),
        out_shape=[jax.ShapeDtypeStruct(shape, jnp.float32) for shape in outs],
        in_specs=[ANY] * len(operands),
        out_specs=[ANY] * len(outs),
        scratch_shapes=[pltpu.SemaphoreType.DMA(n) for n in sems],
        compiler_params=pltpu.CompilerParams(collective_id=ident, has_side_effects=True),
    )(*operands)


def couple_kernel(count, last, ints, reals, *refs):
    if last:
        field, direct, mirror, base, out, pots = refs
    else:
        field, direct, mirror, out, pots = refs
    channels, height, width = field.shape[1:]
    orders = pots.shape[0]
    spacing = 8.0 / count
    row = ints[0] + pl.program_id(0) * height
    row = row + lax.broadcasted_iota(jnp.int32, (height, width), 0)
    col = ints[1] + lax.broadcasted_iota(jnp.int32, (height, width), 1)
    first = row.astype(jnp.float32) * spacing
    second = col.astype(jnp.float32) * spacing
    greater = jnp.maximum(first, second)
    root = jnp.sqrt(greater * greater + 1.0)
    ratio = jnp.minimum(first, second) / root
    pot = 1.0 / root
    for order in range(orders):
        pots[order] = pot
        pot = pot * ratio
    reach = jnp.maximum(row, col)

    def channel(c, carry):
        other = ints[2 + c]
        real_part = direct[0, c] + mirror[0, other]
        imag_part = direct[1, c] + mirror[1, other]
        for order in range(orders):
            k = ints[2 + 2 * channels + c * orders + order]
            c_real = reals[c * orders + order]
            c_imag = reals[channels * orders + c * orders + order]
            pot = pots[order]
            s_real = pot * field[0, k]
            s_imag = pot * field[1, k]
            real_part = real_part + (c_real * s_real - c_imag * s_imag)
            imag_part = imag_part + (c_real * s_imag + c_imag * s_real)
        live = reach < ints[2 + channels + c]
        real_part = jnp.where(live, real_part, 0.0)
        imag_part = jnp.where(live, imag_part, 0.0)
        if last:
            real_part = 2.0 * real_part - base[0, c]
            imag_part = 2.0 * imag_part - base[1, c]
        out[0, c] = real_part
        out[1, c] = imag_part
        return carry

    lax.fori_loop(0, channels, channel, 0)


def couple_tiles(count, ints, reals, orders, arrays):
    last = len(arrays) == 4
    shape = arrays[0].shape
    height = 16
    block = pl.BlockSpec((2, shape[1], height, shape[3]), lambda n: (0, 0, n, 0))
    smem = pl.BlockSpec(memory_space=pltpu.SMEM)
    return pl.pallas_call(
        functools.partial(couple_kernel, count, last),
        grid=(shape[2] // height,),
        out_shape=jax.ShapeDtypeStruct(shape, jnp.float32),
        in_specs=[smem, smem] + [block] * len(arrays),
        out_specs=block,
        scratch_shapes=[pltpu.VMEM((orders, height, shape[3]), jnp.float32)],
    )(ints, reals, *arrays)


def radial_images(radial_op, block):
    image = jnp.einsum("ak,mkb->mab", radial_op, block, precision=lax.Precision.HIGH)
    return image, jnp.swapaxes(image, 1, 2)


def local(wave_field, radial_op, coupling, couple, partner, extent):
    chans = lax.axis_size("chan")
    strips = lax.axis_size("strip")
    per, rows, grid = wave_field.shape[1:]
    width = grid // chans
    orders = coupling.shape[2]
    tiles = (2 * chans, per, rows, width)
    whole = (2, chans * per, rows, width)
    tall = (per, grid, width)
    starts = jnp.stack([lax.axis_index("strip") * rows, lax.axis_index("chan") * width])
    ints = jnp.concatenate([starts.astype(jnp.int32), partner, extent, couple.reshape(-1)])
    reals = coupling.reshape(-1)

    def images(ident, block):
        image, turned = radial_images(radial_op, block)
        _, mirror, direct = exchange(
            image_kernel,
            ident,
            [(strips, per, rows, width), tiles, tiles],
            [(strips,), (strips,), (2 * chans,), (2 * chans,), (2 * chans,), (2 * chans,), (3,)],
            image,
            turned,
        )
        return direct.reshape(whole), mirror.reshape(whole)

    block, field = exchange(
        gather_kernel,
        0,
        [tall, tiles],
        [(strips,), (strips,), (2 * chans,), (2 * chans,), (3,)],
        wave_field.reshape(2 * per, rows, grid),
    )
    field = field.reshape(whole)
    direct, mirror = images(1, block)
    first_step = couple_tiles(grid, ints, reals, orders, (field, direct, mirror))
    _, block = exchange(
        back_kernel,
        2,
        [tiles, tall],
        [(2 * chans,), (2 * chans,), (strips,), (strips,), ()],
        first_step.reshape(tiles),
    )
    direct, mirror = images(1, block)
    second_step = couple_tiles(grid, ints, reals, orders, (first_step, direct, mirror, field))
    return (first_step, second_step)


def dispatch(wave_field, *rest):
    chans = lax.axis_size("chan")
    strips = lax.axis_size("strip")
    width = wave_field.shape[3] // chans
    if strips == 2 * chans and width % 128 == 0 and wave_field.shape[2] % 16 == 0:
        return local(wave_field, *rest)
    return general(wave_field, *rest)


def solution(mesh):
    placed = (P(None, "chan", "strip", None), P(), P(), P(), P(), P())
    return jax.shard_map(
        dispatch,
        mesh=mesh,
        in_specs=placed,
        out_specs=(P(None, None, "strip", "chan"), P(None, None, "strip", "chan")),
        check_vma=False,
    )
```

profile of v0, /device:TPU:9, one launch (start us, length us, event | category | flops | bytes accessed | tf_op | source)
XLA Modules:
  0.0 1206.9 jit_solution(3681979329171622054)
XLA Ops:
  0.6 0.8 copy.13
  1.4 0.1 reshape.31
  1.5 1.3 concatenate.3.ints
  2.8 0.8 copy.14
  3.5 0.6 reshape.32.reals
  4.2 207.3 %shard_map.77 = (f32[4,1536,384]{2,1,0:T(8,128)}, f32[8,4,192,384]{3,2,1,0:T(8,128)}) custom-call(f32[8,192,1536]{2,1,0:T(8,128)} %bitcast.23), custom_call_target="tpu_custom_call" | custom-call | tf_op jit(solution)/shard_map/pallas_call | solution.py:323
  211.5 50.8 %fusion.2.it = f32[4,384,1536]{2,1,0:T(8,128)} fusion(f32[4,1536,384]{2,1,0:T(8,128)} %get-tuple-element.10, f32[1536,1536]{1,0:T(8,128)} %param.7), kind=kOutput, calls=%fused_computation.2 | convolution fusion | flops 21743271936 | bytes 28311552 | tf_op jit(solution)/shard_map/ak,mkb->mab/dot_general | solution.py:398
  262.3 9.6 copy.16
  271.9 283.0 %shard_map.78 = (f32[8,4,192,384]{3,2,1,0:T(8,128)}, f32[8,4,192,384]{3,2,1,0:T(8,128)}, f32[8,4,192,384]{3,2,1,0:T(8,128)}) custom-call(f32[4,1536,384]{2,1,0:T(8,128)} %bitcast.19, f32[4,384,1536]{2,1,0:T(8,128)} %fusion.2.it), custom_call_target="tpu_custom_call" | custom-call | tf_op jit(solution)/shard_map/pallas_call | solution.py:323
  554.9 22.7 %shard_map.79.refs_0_ = f32[2,16,192,384]{3,2,1,0:T(8,128)} custom-call(s32[162]{0:T(256)} %concatenate.3.ints, f32[256]{0:T(256)} %reshape.32.reals, f32[2,16,192,384]{3,2,1,0:T(8,128)} %bitcast.21, f32[2,16,192,384]{3,2,1,0:T(8,128)} %bitcast.27, f32[2,16,192,384]{3,2,1,0:T(8,128)} %bitcast.26), custom_call_target="tpu_custom_call" | custom-call | tf_op jit(solution)/shard_map/pallas_call | solution.py:387
  577.6 233.1 %shard_map.80 = (f32[8,4,192,384]{3,2,1,0:T(8,128)}, f32[4,1536,384]{2,1,0:T(8,128)}) custom-call(f32[8,4,192,384]{3,2,1,0:T(8,128)} %bitcast.18), custom_call_target="tpu_custom_call" | custom-call | tf_op jit(solution)/shard_map/pallas_call | solution.py:323
  810.7 51.0 %fusion.it = f32[4,384,1536]{2,1,0:T(8,128)} fusion(f32[4,1536,384]{2,1,0:T(8,128)} %get-tuple-element.13, f32[1536,1536]{1,0:T(8,128)} %param.7), kind=kOutput, calls=%fused_computation | convolution fusion | flops 21743271936 | bytes 28311552 | tf_op jit(solution)/shard_map/ak,mkb->mab/dot_general | solution.py:398
  861.7 9.6 copy.18
  871.4 310.8 %shard_map.81 = (f32[8,4,192,384]{3,2,1,0:T(8,128)}, f32[8,4,192,384]{3,2,1,0:T(8,128)}, f32[8,4,192,384]{3,2,1,0:T(8,128)}) custom-call(f32[4,1536,384]{2,1,0:T(8,128)} %bitcast.20, f32[4,384,1536]{2,1,0:T(8,128)} %fusion.it), custom_call_target="tpu_custom_call" | custom-call | tf_op jit(solution)/shard_map/pallas_call | solution.py:323
  1182.2 24.8 %shard_map.82 = f32[2,16,192,384]{3,2,1,0:T(8,128)} custom-call(s32[162]{0:T(256)} %concatenate.3.ints, f32[256]{0:T(256)} %reshape.32.reals, f32[2,16,192,384]{3,2,1,0:T(8,128)} %shard_map.79.refs_0_, f32[2,16,192,384]{3,2,1,0:T(8,128)} %bitcast.25, f32[2,16,192,384]{3,2,1,0:T(8,128)} %bitcast.24, f32[2,16,192,384]{3,2,1,0:T(8,128)} %bitcast.22), custom_call_target="tpu_custom_call" | custom-call | tf_op jit(solution)/shard_map/pallas_call | solution.py:387
where the time goes:
time: 1210 us
  Pallas kernels  1080 us (89%)
  matrix products  102 us (8%)
  local copies, waits for them, and re-layouts  22.7 us (2%)
    pallas_call x4, Pallas kernels, exchange(): pl.pallas_call(functools.partial(kernel, chans, strips), out_shape=[jax.S...  1030 us
    dot_general x2, matrix products, radial_images(): jnp.einsum('ak,mkb->mab', radial_op, block, precision=lax.Precision.HIGH)  102 us
    pallas_call x2, Pallas kernels, couple_tiles(): pl.pallas_call(functools.partial(couple_kernel, count, last), grid=(shape...  47.5 us

commit v1 on v0

--- a/solution.py
+++ b/solution.py
@@ -148,176 +148,310 @@
     return pl.ds(pl.multiple_of(block * height, 8), height)
 
 
-def gather_kernel(chans, strips, x, y, f, zs, zr, cs, cr, ls):
+def split(read, high, low, count, step):
+    def one(n, carry):
+        at = pl.ds(pl.multiple_of(n * step, step), step)
+        value = read(at)
+        top = value.astype(jnp.bfloat16)
+        high[at, :] = top
+        low[at, :] = (value - top.astype(jnp.float32)).astype(jnp.bfloat16)
+        return carry
+
+    lax.fori_loop(0, count // step, one, 0)
+
+
+def load_operator(radial, turned, rh, rl, sems):
+    per, width, grid = turned.shape
+    loads = [
+        pltpu.make_async_copy(radial.at[pl.ds(n * width, width), :], turned.at[n], sems.at[n])
+        for n in range(grid // width)
+    ]
+    return loads
+
+
+def split_operator(loads, turned, rh, rl):
+    width = turned.shape[1]
+    for n, load in enumerate(loads):
+        load.wait()
+        split(
+            lambda at, n=n: turned[n, at, :],
+            rh.at[pl.ds(n * width, width), :],
+            rl.at[pl.ds(n * width, width), :],
+            width,
+            32,
+        )
+
+
+def product(j, y, img, turned, rh, rl, yh, yl):
+    grid = y.shape[1]
+    step = 256
+    split(lambda at: y[j, at, :], yh, yl, grid, 64)
+
+    def one(n, carry):
+        at = pl.ds(pl.multiple_of(n * step, step), step)
+        top = rh[at, :]
+        total = jnp.dot(top, yh[...], preferred_element_type=jnp.float32)
+        total = total + jnp.dot(top, yl[...], preferred_element_type=jnp.float32)
+        total = total + jnp.dot(rl[at, :], yh[...], preferred_element_type=jnp.float32)
+        img[j, at, :] = total
+        turned[j, :, at] = total.T
+        return carry
+
+    lax.fori_loop(0, grid // step, one, 0)
+
+
+def far_order(strips):
+    half = strips // 2
+    return sorted(range(1, strips), key=lambda d: (abs(d - half), d))
+
+
+def chunks(per, body):
+    def one(j, carry):
+        body(j)
+        return carry
+
+    lax.fori_loop(0, per, one, 0)
+
+
+class Spread:
+    def __init__(self, c, s, chans, strips, img, turned, w, mt, dd, sems):
+        self.c, self.s, self.chans, self.strips = c, s, chans, strips
+        self.img, self.turned, self.w, self.mt, self.dd = img, turned, w, mt, dd
+        self.zs, self.zr, self.ms, self.mr, self.fs, self.fr, self.ls = sems
+        self.rows = w.shape[2]
+        self.width = w.shape[3]
+        self.member = rem(s, 2)
+        group = s // 2
+        self.ring = [(c, rem(s + d, strips)) for d in range(1, strips)]
+        self.plane = [
+            (rem(c + r, chans), group * 2 + rem(self.member + e, 2))
+            for r in range(chans)
+            for e in range(2)
+        ]
+
+    def hop(self, j, d):
+        t = self.ring[d - 1][1]
+        return remote(
+            self.img.at[j, lines(t, self.rows), :],
+            self.w.at[j, self.s],
+            self.zs.at[j, d],
+            self.zr.at[j, d],
+            self.ring[d - 1],
+        )
+
+    def mirror(self, j, k):
+        slot = self.member * self.chans + self.c
+        to = self.plane[k][0]
+        m = rem(self.member + k % 2, 2)
+        part = self.turned.at[j, lines(m, self.rows), columns(to, self.width)]
+        if k == 0:
+            return pltpu.make_async_copy(part, self.mt.at[slot, j], self.ls.at[j, 2])
+        return remote(
+            part, self.mt.at[slot, j], self.ms.at[j, k], self.mr.at[j, k], self.plane[k]
+        )
+
+    def forward(self, source, j, u):
+        to = u // 2
+        p = rem(u, 2)
+        away = rem(to - self.c + self.chans, self.chans)
+        target = self.dd.at[p * self.chans + self.c, j]
+
+        @pl.when(away == 0)
+        def _():
+            pltpu.make_async_copy(source, target, self.ls.at[j, p]).start()
+
+        @pl.when(away != 0)
+        def _():
+            k = away * 2 + p
+            remote(source, target, self.fs.at[j, k], self.fr.at[j, k], (to, self.s)).start()
+
+    def start(self, j):
+        for d in far_order(self.strips):
+            self.hop(j, d).start()
+        for k in reversed(range(2 * self.chans)):
+            self.mirror(j, k).start()
+
+    def relay(self, j):
+        self.forward(self.img.at[j, lines(self.s, self.rows), :], j, self.s)
+        for d in far_order(self.strips)[::-1]:
+            self.hop(j, d).wait_recv()
+            u = rem(self.s - d + self.strips, self.strips)
+            self.forward(self.w.at[j, u], j, u)
+
+    def finish(self, j):
+        for d in range(1, self.strips):
+            self.hop(j, d).wait_send()
+        for k in range(2 * self.chans):
+            self.mirror(j, k).wait()
+        for p in range(2):
+            own = self.dd.at[p * self.chans + self.c, j]
+            pltpu.make_async_copy(self.w.at[j, 0], own, self.ls.at[j, p]).wait()
+            for r in range(1, self.chans):
+                k = r * 2 + p
+                sender = rem(self.c - r + self.chans, self.chans)
+                remote(
+                    self.w.at[j, 0],
+                    self.dd.at[p * self.chans + sender, j],
+                    self.fs.at[j, k],
+                    self.fr.at[j, k],
+                    (rem(self.c + r, self.chans), self.s),
+                ).wait()
+
+
+def first_kernel(
+    chans, strips, x, radial, f, mt, dd, y, img, turned, w, rh, rl, yh, yl,
+    gs, gr, gl, cs, cr, cl, rs, zs, zr, ms, mr, fs, fr, ls,
+):
+    c = lax.axis_index("chan")
+    s = lax.axis_index("strip")
+    per, _, width = y.shape
+    rows = x.shape[1]
+    spread = Spread(c, s, chans, strips, img, turned, w, mt, dd, (zs, zr, ms, mr, fs, fr, ls))
+    greet(spread.ring + spread.plane[2:])
+
+    def gather(j, d):
+        t = spread.ring[d - 1][1]
+        return remote(
+            x.at[rem(t, 2) * per + j, :, columns(t // 2, width)],
+            y.at[j, lines(s, rows), :],
+            gs.at[j, d],
+            gr.at[j, d],
+            spread.ring[d - 1],
+        )
+
+    def keep(j):
+        return pltpu.make_async_copy(
+            x.at[rem(s, 2) * per + j, :, columns(s // 2, width)],
+            y.at[j, lines(s, rows), :],
+            gl.at[j],
+        )
+
+    def field(p, r):
+        to = rem(c + r, chans)
+        part = x.at[pl.ds(p * per, per), :, columns(to, width)]
+        target = f.at[p * chans + c]
+        if r == 0:
+            return pltpu.make_async_copy(part, target, cl.at[p])
+        return remote(part, target, cs.at[r * 2 + p], cr.at[r * 2 + p], (to, s))
+
+    def begin(j):
+        for d in far_order(strips):
+            gather(j, d).start()
+        keep(j).start()
+
+    fields = [field(p, r) for r in range(chans) for p in range(2)]
+    loads = load_operator(radial, turned, rh, rl, rs)
+    chunks(per, begin)
+    for load in loads:
+        load.start()
+    for copy in fields:
+        copy.start()
+    split_operator(loads, turned, rh, rl)
+
+    def work(j):
+        keep(j).wait()
+        for d in range(1, strips):
+            gather(j, d).wait_recv()
+        product(j, y, img, turned, rh, rl, yh, yl)
+        spread.start(j)
+
+    chunks(per, work)
+    chunks(per, spread.relay)
+
+    def finish(j):
+        for d in range(1, strips):
+            gather(j, d).wait_send()
+        spread.finish(j)
+
+    for copy in fields:
+        copy.wait()
+    chunks(per, finish)
+
+
+def second_kernel(
+    chans, strips, v, radial, b, mt, dd, y, img, turned, w, rh, rl, yh, yl,
+    bs, br, gs, gr, gl, rs, zs, zr, ms, mr, fs, fr, ls,
+):
     c = lax.axis_index("chan")
     s = lax.axis_index("strip")
     per = y.shape[0]
-    width = y.shape[2]
-    rows = x.shape[1]
-    ring = [(c, rem(s + d, strips)) for d in range(1, strips)]
-    plane = [(rem(c + r, chans), s) for r in range(1, chans)]
-    greet(ring + plane)
-    copies = []
-    for d in range(1, strips):
-        t = ring[d - 1][1]
-        copies.append(
-            remote(
-                x.at[pl.ds(rem(t, 2) * per, per), :, columns(t // 2, width)],
-                y.at[:, lines(s, rows), :],
-                zs.at[d],
-                zr.at[d],
-                ring[d - 1],
-            )
+    rows = v.shape[2]
+    spread = Spread(c, s, chans, strips, img, turned, w, mt, dd, (zs, zr, ms, mr, fs, fr, ls))
+    greet(spread.ring + spread.plane[2:])
+
+    def back(j, r, p):
+        to = rem(c + r, chans)
+        k = r * 2 + p
+        return remote(
+            v.at[p * chans + to, j], b.at[p * chans + c, j], bs.at[j, k], br.at[j, k], (to, s)
         )
-    for r in range(1, chans):
-        j = plane[r - 1][0]
-        for p in range(2):
-            copies.append(
-                remote(
-                    x.at[pl.ds(p * per, per), :, columns(j, width)],
-                    f.at[p * chans + c],
-                    cs.at[r * 2 + p],
-                    cr.at[r * 2 + p],
-                    plane[r - 1],
-                )
-            )
-    copies.append(
-        pltpu.make_async_copy(
-            x.at[pl.ds(rem(s, 2) * per, per), :, columns(s // 2, width)],
-            y.at[:, lines(s, rows), :],
-            ls.at[0],
-        )
-    )
-    for p in range(2):
-        copies.append(
-            pltpu.make_async_copy(
-                x.at[pl.ds(p * per, per), :, columns(c, width)], f.at[p * chans + c], ls.at[1 + p]
-            )
-        )
-    for copy in copies:
-        copy.start()
-    for copy in copies:
-        copy.wait()
-
-
-def image_kernel(chans, strips, i, it, w, mt, dd, zs, zr, ms, mr, fs, fr, ls):
-    c = lax.axis_index("chan")
-    s = lax.axis_index("strip")
-    rows = w.shape[2]
-    width = w.shape[3]
-    group = s // 2
-    member = rem(s, 2)
-    ring = [(c, rem(s + d, strips)) for d in range(1, strips)]
-    plane = [
-        (rem(c + r, chans), group * 2 + rem(member + e, 2))
-        for r in range(chans)
-        for e in range(2)
-    ]
-    greet(ring + plane[2:])
-    slot = member * chans + c
-    hops = []
-    for d in range(1, strips):
-        t = ring[d - 1][1]
-        hops.append(
-            remote(i.at[:, lines(t, rows), :], w.at[s], zs.at[d], zr.at[d], ring[d - 1])
-        )
-
-    def mirror(k):
-        j = plane[k][0]
-        m = rem(member + k % 2, 2)
-        part = it.at[:, lines(m, rows), columns(j, width)]
-        if k == 0:
-            return pltpu.make_async_copy(part, mt.at[slot], ls.at[2])
-        return remote(part, mt.at[slot], ms.at[k], mr.at[k], plane[k])
-
-    mirrors = [mirror(k) for k in range(2 * chans)]
-    for hop in hops:
-        hop.start()
-
-    def forward(source, u):
-        j = u // 2
-        p = rem(u, 2)
-        away = rem(j - c + chans, chans)
+
+    def forward(source, j, block, p):
+        t = block * 2 + p
+        away = rem(t - s + strips, strips)
+        target = y.at[j, lines(s, rows), :]
 
         @pl.when(away == 0)
         def _():
-            pltpu.make_async_copy(source, dd.at[p * chans + c], ls.at[p]).start()
+            pltpu.make_async_copy(source, target, gl.at[j]).start()
 
         @pl.when(away != 0)
         def _():
-            k = away * 2 + p
-            remote(source, dd.at[p * chans + c], fs.at[k], fr.at[k], (j, s)).start()
-
-    forward(i.at[:, lines(s, rows), :], s)
-    for copy in mirrors:
-        copy.start()
-    for d in range(1, strips):
-        hops[d - 1].wait_recv()
+            remote(source, target, gs.at[j, away], gr.at[j, away], (c, t)).start()
+
+    def begin(j):
+        for r in reversed(range(1, chans)):
+            for p in range(2):
+                back(j, r, p).start()
+
+    def relay(j):
+        for p in range(2):
+            forward(v.at[p * chans + c, j], j, c, p)
+        for r in reversed(range(1, chans)):
+            sender = rem(c - r + chans, chans)
+            for p in range(2):
+                back(j, r, p).wait_recv()
+                forward(b.at[p * chans + sender, j], j, sender, p)
+
+    loads = load_operator(radial, turned, rh, rl, rs)
+    chunks(per, begin)
+    for load in loads:
+        load.start()
+    chunks(per, relay)
+    split_operator(loads, turned, rh, rl)
+
+    def arrive(j, d):
         u = rem(s - d + strips, strips)
-        forward(w.at[u], u)
-    for hop in hops:
-        hop.wait_send()
-    for copy in mirrors:
-        copy.wait()
-    for p in range(2):
-        pltpu.make_async_copy(w.at[0], dd.at[p * chans + c], ls.at[p]).wait()
+        return remote(
+            v.at[0, 0],
+            y.at[j, lines(u, rows), :],
+            gs.at[j, d],
+            gr.at[j, d],
+            spread.ring[d - 1],
+        )
+
+    def work(j):
+        pltpu.make_async_copy(v.at[0, 0], y.at[j, lines(s, rows), :], gl.at[j]).wait()
+        for d in range(1, strips):
+            arrive(j, d).wait_recv()
+        product(j, y, img, turned, rh, rl, yh, yl)
+        spread.start(j)
+
+    chunks(per, work)
+    chunks(per, spread.relay)
+
+    def finish(j):
         for r in range(1, chans):
-            k = r * 2 + p
-            from_chan = rem(c - r + chans, chans)
-            remote(
-                w.at[0], dd.at[p * chans + from_chan], fs.at[k], fr.at[k], (rem(c + r, chans), s)
-            ).wait()
-
-
-def back_kernel(chans, strips, v, w, y, cs, cr, zs, zr, ls):
-    c = lax.axis_index("chan")
-    s = lax.axis_index("strip")
-    rows = v.shape[2]
-    ring = [(c, rem(s + d, strips)) for d in range(1, strips)]
-    plane = [(rem(c + r, chans), s) for r in range(1, chans)]
-    greet(ring + plane)
-    hops = {}
-    for r in range(1, chans):
-        j = plane[r - 1][0]
-        for p in range(2):
-            k = r * 2 + p
-            hops[k] = remote(
-                v.at[p * chans + j], w.at[p * chans + c], cs.at[k], cr.at[k], plane[r - 1]
-            )
-            hops[k].start()
-
-    def forward(source, j, p):
-        t = j * 2 + p
-        away = rem(t - s + strips, strips)
-
-        @pl.when(away == 0)
-        def _():
-            pltpu.make_async_copy(source, y.at[:, lines(s, rows), :], ls).start()
-
-        @pl.when(away != 0)
-        def _():
-            remote(
-                source, y.at[:, lines(s, rows), :], zs.at[away], zr.at[away], (c, t)
-            ).start()
-
-    for p in range(2):
-        forward(v.at[p * chans + c], c, p)
-    for r in range(1, chans):
-        j = rem(c - r + chans, chans)
-        for p in range(2):
-            hops[r * 2 + p].wait_recv()
-            forward(w.at[p * chans + j], j, p)
-    for k in hops:
-        hops[k].wait_send()
-    pltpu.make_async_copy(v.at[0], y.at[:, lines(s, rows), :], ls).wait()
-    for d in range(1, strips):
-        u = rem(s - d + strips, strips)
-        remote(
-            v.at[0], y.at[:, lines(u, rows), :], zs.at[d], zr.at[d], (c, rem(s + d, strips))
-        ).wait()
-
-
-def exchange(kernel, ident, outs, sems, *operands):
+            for p in range(2):
+                back(j, r, p).wait_send()
+        for d in range(1, strips):
+            arrive(j, d).wait_send()
+        spread.finish(j)
+
+    chunks(per, finish)
+
+
+def exchange(kernel, ident, outs, buffers, sems, *operands):
     chans = lax.axis_size("chan")
     strips = lax.axis_size("strip")
     return pl.pallas_call(
@@ -325,8 +459,11 @@
         out_shape=[jax.ShapeDtypeStruct(shape, jnp.float32) for shape in outs],
         in_specs=[ANY] * len(operands),
         out_specs=[ANY] * len(outs),
-        scratch_shapes=[pltpu.SemaphoreType.DMA(n) for n in sems],
-        compiler_params=pltpu.CompilerParams(collective_id=ident, has_side_effects=True),
+        scratch_shapes=[pltpu.VMEM(*buffer) for buffer in buffers]
+        + [pltpu.SemaphoreType.DMA(n) for n in sems],
+        compiler_params=pltpu.CompilerParams(
+            collective_id=ident, has_side_effects=True, vmem_limit_bytes=60 * 2**20
+        ),
     )(*operands)
 
 
@@ -394,11 +531,6 @@
     )(ints, reals, *arrays)
 
 
-def radial_images(radial_op, block):
-    image = jnp.einsum("ak,mkb->mab", radial_op, block, precision=lax.Precision.HIGH)
-    return image, jnp.swapaxes(image, 1, 2)
-
-
 def local(wave_field, radial_op, coupling, couple, partner, extent):
     chans = lax.axis_size("chan")
     strips = lax.axis_size("strip")
@@ -407,42 +539,47 @@
     orders = coupling.shape[2]
     tiles = (2 * chans, per, rows, width)
     whole = (2, chans * per, rows, width)
-    tall = (per, grid, width)
     starts = jnp.stack([lax.axis_index("strip") * rows, lax.axis_index("chan") * width])
     ints = jnp.concatenate([starts.astype(jnp.int32), partner, extent, couple.reshape(-1)])
     reals = coupling.reshape(-1)
-
-    def images(ident, block):
-        image, turned = radial_images(radial_op, block)
-        _, mirror, direct = exchange(
-            image_kernel,
-            ident,
-            [(strips, per, rows, width), tiles, tiles],
-            [(strips,), (strips,), (2 * chans,), (2 * chans,), (2 * chans,), (2 * chans,), (3,)],
-            image,
-            turned,
-        )
-        return direct.reshape(whole), mirror.reshape(whole)
-
-    block, field = exchange(
-        gather_kernel,
+    buffers = [
+        ((per, grid, width), jnp.float32),
+        ((per, grid, width), jnp.float32),
+        ((per, width, grid), jnp.float32),
+        ((per, strips, rows, width), jnp.float32),
+        ((grid, grid), jnp.bfloat16),
+        ((grid, grid), jnp.bfloat16),
+        ((grid, width), jnp.bfloat16),
+        ((grid, width), jnp.bfloat16),
+    ]
+    ring = (per, strips)
+    plane = (per, 2 * chans)
+    spread = [(chans,), ring, ring, plane, plane, plane, plane, (per, 3)]
+    field, mirror, direct = exchange(
+        first_kernel,
         0,
-        [tall, tiles],
-        [(strips,), (strips,), (2 * chans,), (2 * chans,), (3,)],
+        [tiles, tiles, tiles],
+        buffers,
+        [ring, ring, (per,), (2 * chans,), (2 * chans,), (2,)] + spread,
         wave_field.reshape(2 * per, rows, grid),
+        radial_op,
     )
     field = field.reshape(whole)
-    direct, mirror = images(1, block)
-    first_step = couple_tiles(grid, ints, reals, orders, (field, direct, mirror))
-    _, block = exchange(
-        back_kernel,
-        2,
-        [tiles, tall],
-        [(2 * chans,), (2 * chans,), (strips,), (strips,), ()],
+    first_step = couple_tiles(
+        grid, ints, reals, orders, (field, direct.reshape(whole), mirror.reshape(whole))
+    )
+    _, mirror, direct = exchange(
+        second_kernel,
+        1,
+        [tiles, tiles, tiles],
+        buffers,
+        [plane, plane, ring, ring, (per,)] + spread,
         first_step.reshape(tiles),
-    )
-    direct, mirror = images(1, block)
-    second_step = couple_tiles(grid, ints, reals, orders, (first_step, direct, mirror, field))
+        radial_op,
+    )
+    second_step = couple_tiles(
+        grid, ints, reals, orders, (first_step, direct.reshape(whole), mirror.reshape(whole), field)
+    )
     return (first_step, second_step)
 
 
@@ -450,7 +587,9 @@
     chans = lax.axis_size("chan")
     strips = lax.axis_size("strip")
     width = wave_field.shape[3] // chans
-    if strips == 2 * chans and width % 128 == 0 and wave_field.shape[2] % 16 == 0:
+    grid = wave_field.shape[3]
+    per_fits = wave_field.shape[1] == chans
+    if strips == 2 * chans and width % 128 == 0 and grid % 256 == 0 and wave_field.shape[2] % 16 == 0 and per_fits:
         return local(wave_field, *rest)
     return general(wave_field, *rest)
 

time: 1210 us -> 944 us (0.78)
  Pallas kernels: 1080 us -> 932 us
  matrix products: 102 us -> 0 us
  local copies, waits for them, and re-layouts: 22.7 us -> 3.53 us
    pallas_call x4 -> x2, Pallas kernels: 1030 us -> 885 us  [exchange(): pl.pallas_call(functools.partial(kernel, chans, strips), out_shape=[jax.S...]
    dot_general x2 -> x0, matrix products: 102 us -> none  [radial_images(): jnp.einsum('ak,mkb->mab', radial_op, block, precision=lax.Precision.HIGH)]
    dot_general x2 -> x0, local copies, waits for them, and re-layouts: 19.2 us -> none  [radial_images(): jnp.einsum('ak,mkb->mab', radial_op, block, precision=lax.Precision.HIGH)]
where the time goes in v1:
time: 944 us; the launch traced here: 936 us
  Pallas kernels  932 us (99%)
    pallas_call x2, Pallas kernels, exchange(): pl.pallas_call(functools.partial(kernel, chans, strips), out_shape=[jax.S...  885 us
    pallas_call x2, Pallas kernels, couple_tiles(): pl.pallas_call(functools.partial(couple_kernel, count, last), grid=(shape...  47.5 us

profile of v1, /device:TPU:9, one launch (start us, length us, event | category | flops | bytes accessed | tf_op | source)
XLA Modules:
  0.0 936.5 jit_solution(3648007999438633647)
XLA Ops:
  0.6 0.8 copy.9
  1.4 0.1 reshape.31
  1.5 1.3 concatenate.3.ints
  2.8 0.8 copy.10
  3.5 0.6 reshape.32.reals
  4.2 433.5 %shard_map.77 = (f32[8,4,192,384]{3,2,1,0:T(8,128)}, f32[8,4,192,384]{3,2,1,0:T(8,128)}, f32[8,4,192,384]{3,2,1,0:T(8,128)}) custom-call(f32[8,192,1536]{2,1,0:T(8,128)} %bitcast.12, f32[1536,1536]{1,0:T(8,128)} %radial.3), custom_call_target="tpu_custom_call" | custom-call | tf_op jit(solution)/shard_map/pallas_call | solution.py:457
  437.7 22.7 %shard_map.78.refs_0_ = f32[2,16,192,384]{3,2,1,0:T(8,128)} custom-call(s32[162]{0:T(256)} %concatenate.3.ints, f32[256]{0:T(256)} %reshape.32.reals, f32[2,16,192,384]{3,2,1,0:T(8,128)} %bitcast.10, f32[2,16,192,384]{3,2,1,0:T(8,128)} %bitcast.16, f32[2,16,192,384]{3,2,1,0:T(8,128)} %bitcast.15), custom_call_target="tpu_custom_call" | custom-call | tf_op jit(solution)/shard_map/pallas_call | solution.py:524
  460.4 451.3 %shard_map.79 = (f32[8,4,192,384]{3,2,1,0:T(8,128)}, f32[8,4,192,384]{3,2,1,0:T(8,128)}, f32[8,4,192,384]{3,2,1,0:T(8,128)}) custom-call(f32[8,4,192,384]{3,2,1,0:T(8,128)} %bitcast.9, f32[1536,1536]{1,0:T(8,128)} %radial.3), custom_call_target="tpu_custom_call" | custom-call | tf_op jit(solution)/shard_map/pallas_call | solution.py:457
  911.7 24.8 %shard_map.80 = f32[2,16,192,384]{3,2,1,0:T(8,128)} custom-call(s32[162]{0:T(256)} %concatenate.3.ints, f32[256]{0:T(256)} %reshape.32.reals, f32[2,16,192,384]{3,2,1,0:T(8,128)} %shard_map.78.refs_0_, f32[2,16,192,384]{3,2,1,0:T(8,128)} %bitcast.14, f32[2,16,192,384]{3,2,1,0:T(8,128)} %bitcast.13, f32[2,16,192,384]{3,2,1,0:T(8,128)} %bitcast.11), custom_call_target="tpu_custom_call" | custom-call | tf_op jit(solution)/shard_map/pallas_call | solution.py:524
